TPU v7x, 512 devices: a whole 4x8x8 slice. The times are simulated.
512 devices in a mesh: ctx: 64 (over z_lo, y, core), head: 8 (over x, z_hi).
Axes of the slice: x: 4, y: 8, z: 8 (z_hi: 2, z_lo: 4; z = z_hi * 4 + z_lo), core: 2. Of those that a mesh axis runs over, the one named last changes fastest.
Arguments:
- tokens: bfloat16 [32768, 3840], P('ctx', 'head'), may hold values from -18 to 18
- w_query: bfloat16 [3840, 4096], P('ctx', 'head'), may hold values from -0.09375 to 0.09375
- key_matrix: bfloat16 [3840, 2048], P('ctx', 'head'), may hold values from -0.09375 to 0.09375
- value_matrix: bfloat16 [3840, 2048], P('ctx', 'head'), may hold values from -0.09375 to 0.09375
- d_attended: bfloat16 [32768, 4096], P('ctx', 'head'), may hold values from -6 to 6
- doc_lengths: int32 [32], replicated, may hold values from 1 to 2048, 32768 in all
Outputs:
- attended: bfloat16 [32768, 4096], P('ctx', 'head')
- key_grad: bfloat16 [32768, 2048], P('ctx', 'head')
Inputs may be any that keep to these rules, and one draw needn't show every extreme that they name: `doc_lengths`: the documents lie end to end from position 0 and fill all 32768 positions.
All inputs are finite; a program needn't handle non-finite values.
Results may differ from a plain program's by a relative error of at most 0.012.
The roundings to bfloat16 on the way count: a program that leaves them out, or rounds other values in their place, can miss the bound.
Values may be sent and summed in bfloat16 or wider, within the bound.
No kernel may reach another device: no remote copies, remote signals or barrier semaphores. Data moves between devices by JAX's collectives and lax.ppermute only.
A program may use at most 64 MiB of HBM per device.

v0:
```python
import jax
import jax.numpy as jnp
from jax import lax
from jax.sharding import PartitionSpec as P

HEAD_SIZE = 256
WINDOW = 1024


def from_behind(block, axis, distance):
    devices = range(lax.axis_size(axis))
    route = [(i - distance, i) for i in devices if i - distance in devices]
    return lax.ppermute(block, axis, route)


def doc_begin(positions, doc_start):
    inside = doc_start[None, :] <= positions[:, None]
    return jnp.max(jnp.where(inside, doc_start[None, :], 0), axis=1)


def add_rows(features, piece):
    return jnp.dot(features, piece, preferred_element_type=jnp.float32)


def attend_local(query, key_ext, value_ext, grad_rows, leading_row, doc_start, kv_heads):
    rows = query.shape[0]
    window_length = key_ext.shape[0]
    width = key_ext.shape[1] // kv_heads
    group = query.shape[1] // (kv_heads * width)
    query_pos = leading_row + jnp.arange(rows, dtype=jnp.int32)
    key_pos = leading_row - (window_length - rows) + jnp.arange(window_length, dtype=jnp.int32)
    begins = doc_begin(query_pos, doc_start)
    allowed = (
        (key_pos[None, :] >= begins[:, None])
        & (key_pos[None, :] <= query_pos[:, None])
        & (key_pos[None, :] > query_pos[:, None] - WINDOW)
    )
    query_four = query.reshape(rows, kv_heads, group, width)
    grad_four = grad_rows.reshape(rows, kv_heads, group, width)
    key_three = key_ext.reshape(window_length, kv_heads, width)
    value_three = value_ext.reshape(window_length, kv_heads, width)
    scores = jnp.einsum("tgeh,sgh->gets", query_four, key_three, preferred_element_type=jnp.float32)
    scores = jnp.where(allowed[None, None], scores, -1e30)
    peak = jnp.max(scores, axis=-1, keepdims=True)
    expo = jnp.exp(scores - peak)
    probs = expo / jnp.sum(expo, axis=-1, keepdims=True)
    probs_low = probs.astype(jnp.bfloat16)
    attended = jnp.einsum(
        "gets,sgh->tgeh", probs_low, value_three, preferred_element_type=jnp.float32
    )
    attended = attended.astype(jnp.bfloat16).reshape(rows, kv_heads * group * width)
    dprob = jnp.einsum("tgeh,sgh->gets", grad_four, value_three, preferred_element_type=jnp.float32)
    delta = jnp.sum(probs * dprob, axis=-1, keepdims=True)
    dscore = (probs * (dprob - delta)).astype(jnp.bfloat16)
    key_part = jnp.einsum("gets,tgeh->sgh", dscore, query_four, preferred_element_type=jnp.float32)
    return (attended, key_part.reshape(window_length, kv_heads * width))


def local(tokens, w_query, key_matrix, value_matrix, d_attended, doc_lengths):
    features = lax.all_gather(tokens, "head", axis=1, tiled=True)
    rows_here = features.shape[0]
    kv_width = key_matrix.shape[1]
    kv_heads = kv_width // HEAD_SIZE

    def add_one(piece):
        return add_rows(features, piece)

    query_sum = add_one(lax.all_gather(w_query, "ctx", axis=0, tiled=True))
    key_sum = add_one(lax.all_gather(key_matrix, "ctx", axis=0, tiled=True))
    value_sum = add_one(lax.all_gather(value_matrix, "ctx", axis=0, tiled=True))
    query = (query_sum * 0.0625).astype(jnp.bfloat16)
    joined = jnp.concatenate([key_sum.astype(jnp.bfloat16), value_sum.astype(jnp.bfloat16)], axis=1)
    blocks = WINDOW // rows_here
    earlier = [from_behind(joined, "ctx", distance) for distance in range(blocks, 0, -1)]
    extended = jnp.concatenate(earlier + [joined], axis=0)
    doc_start = jnp.cumsum(doc_lengths) - doc_lengths
    leading_row = lax.axis_index("ctx") * rows_here
    attended, key_part = attend_local(
        query,
        extended[:, :kv_width],
        extended[:, kv_width:],
        d_attended,
        leading_row,
        doc_start,
        kv_heads,
    )

    def share(distance):
        begin = (blocks - distance) * rows_here
        return key_part[begin : begin + rows_here]

    key_total = share(0)
    for distance in range(1, blocks + 1):
        key_total = key_total + from_behind(share(distance), "ctx", -distance)
    key_grad = key_total.astype(jnp.bfloat16)
    return (attended, key_grad)


def solution(mesh):
    return jax.shard_map(
        local,
        mesh=mesh,
        in_specs=(
            P("ctx", "head"),
            P("ctx", "head"),
            P("ctx", "head"),
            P("ctx", "head"),
            P("ctx", "head"),
            P(),
        ),
        out_specs=(P("ctx", "head"), P("ctx", "head")),
        check_vma=False,
    )
```

profile of v0, /device:TPU:24, one launch (start us, length us, event | category | flops | bytes accessed | tf_op | source)
XLA Modules:
  0.0 539.3 jit_solution(11671990753732700113)
XLA Ops:
  7.2 0.0 all-gather.10.cloned.1.call-start
  7.2 0.7 all-gather.10.cloned.1.call-update
  7.9 0.0 all-gather.12.cloned.1.call-start
  7.9 0.7 all-gather.12.cloned.1.call-update
  8.6 0.0 all-gather.8.cloned.1.call-start
  8.7 0.7 all-gather.8.cloned.1.call-update
  9.4 0.0 all-gather.14.cloned.1.call-start
  9.4 0.5 all-gather.14.cloned.1.call-update
  10.0 0.7 copy.35
  10.7 0.1 reduce-window.9
  10.8 0.1 reduce.3
  10.9 0.7 sub.27
  11.5 0.1 select_reduce_fusion
  11.6 119.0 %all-gather.10.cloned.1.call-done = bf16[64,60,256]{2,1,0:T(8,128)(2,1)} async-done(((bf16[1,60,256]{2,1,0:T(8,128)(2,1)}), bf16[64,60,256]{2,1,0:T(8,128)(2,1)}) %all-gather.10.cloned.1.call-update) | async-done | bytes 1966096 | tf_op jit(solution)/shard_map/all_gather | solution.py:69
  130.7 2.5 reshape.188
  133.1 115.6 %all-gather.12.cloned.1.call-done = bf16[64,60,256]{2,1,0:T(8,128)(2,1)} async-done(((bf16[1,60,256]{2,1,0:T(8,128)(2,1)}), bf16[64,60,256]{2,1,0:T(8,128)(2,1)}) %all-gather.12.cloned.1.call-update) | async-done | bytes 1966096 | tf_op jit(solution)/shard_map/all_gather | solution.py:70
  248.7 3.8 reshape.190
  252.5 108.1 %all-gather.8.cloned.1.call-done = bf16[512,3840]{0,1:T(8,128)(2,1)} async-done(((bf16[512,480]{0,1:T(8,128)(2,1)}), bf16[512,3840]{0,1:T(8,128)(2,1)}) %all-gather.8.cloned.1.call-update) | async-done | bytes 3932176 | tf_op jit(solution)/shard_map/all_gather | solution.py:60
  360.6 3.5 convolution_convert_fusion.1
  364.0 0.0 copy-done
  364.1 0.4 copy-done.2
  364.4 1.2 convolution_convert_fusion
  365.7 1.9 collective-permute-start.1
  367.6 4.8 collective-permute-start
  372.4 1.2 compare_and_fusion
  373.6 7.6 %collective-permute-done.1 = bf16[512,512]{0,1:T(8,128)(2,1)S(1)} collective-permute-done((bf16[512,512]{0,1:T(8,128)(2,1)S(1)}, bf16[512,512]{0,1:T(8,128)(2,1)S(1)}, u32[]{:S(2)}, u32[]{:S(2)}) %collective-permute-start.1) | collective-permute-done | bytes 524320 | tf_op jit(solution)/shard_map/ppermute | solution.py:13
  381.3 6.2 %collective-permute-done = bf16[512,512]{0,1:T(8,128)(2,1)S(1)} collective-permute-done((bf16[512,512]{0,1:T(8,128)(2,1)S(1)}, bf16[512,512]{0,1:T(8,128)(2,1)S(1)}, u32[]{:S(2)}, u32[]{:S(2)}) %collective-permute-start) | collective-permute-done | bytes 524320 | tf_op jit(solution)/shard_map/ppermute | solution.py:13
  387.4 0.1 maximum_maximum_fusion
  387.5 99.0 %all-gather.14.cloned.1.call-done = bf16[64,60,512]{2,1,0:T(8,128)(2,1)} async-done(((bf16[1,60,512]{2,1,0:T(8,128)(2,1)}), bf16[64,60,512]{2,1,0:T(8,128)(2,1)}) %all-gather.14.cloned.1.call-update) | async-done | bytes 3932176 | tf_op jit(solution)/shard_map/all_gather | solution.py:68
  486.5 6.3 %reshape.192 = bf16[3840,512]{1,0:T(8,128)(2,1)} reshape(bf16[64,60,512]{2,1,0:T(8,128)(2,1)} %all-gather.14.cloned.1.call-done) | data formatting | bytes 7864320
  492.9 5.5 %fusion.21 = bf16[512,512]{0,1:T(8,128)(2,1)S(1)} fusion(bf16[512,3840]{0,1:T(8,128)(2,1)} %all-gather.8.cloned.1.call-done, bf16[3840,512]{1,0:T(8,128)(2,1)} %reshape.192), kind=kOutput, calls=%fused_computation.21 | convolution fusion | flops 2013790208 | bytes 8388608 | tf_op jit(solution)/shard_map/dot_general | solution.py:22
  498.4 1.3 fusion.3
  499.7 0.0 copy-start.3
  499.7 1.3 fusion.5
  501.0 0.0 copy-done.3
  501.0 2.5 fusion
  503.5 2.5 fusion.13
  506.1 0.0 copy-start.1
  506.1 1.1 slice_bitcast_fusion.6
  507.2 2.0 collective-permute-start.2
  509.2 2.5 collective-permute-start.3
  511.7 3.0 fusion.18
  514.6 0.0 copy-done.1
  514.6 2.0 copy.42
  516.7 3.4 collective-permute-done.2
  520.1 10.7 %collective-permute-done.3 = f32[512,256]{0,1:T(8,128)S(1)} collective-permute-done((f32[512,256]{0,1:T(8,128)}, f32[512,256]{0,1:T(8,128)S(1)}, u32[]{:S(2)}, u32[]{:S(2)}) %collective-permute-start.3) | collective-permute-done | bytes 524320 | tf_op jit(solution)/shard_map/ppermute | solution.py:13
  530.8 1.2 fusion.28
  531.9 0.8 copy.43
  (5 shorter events, 0.1 us)
Async XLA Ops:
  7.2 123.5 %all-gather.10.cloned.1.call-start = ((), (), s32[]{:S(2)}) async-start(), calls=%async_computation.1 | async-start | bytes 2129920 | tf_op jit(solution)/shard_map/all_gather | solution.py:69
  7.9 240.8 %all-gather.12.cloned.1.call-start = ((), (), s32[]{:S(2)}) async-start(), calls=%async_computation.2 | async-start | bytes 2129920 | tf_op jit(solution)/shard_map/all_gather | solution.py:70
  8.6 351.9 %all-gather.8.cloned.1.call-start = ((), (), s32[]{:S(2)}) async-start(), calls=%async_computation | async-start | bytes 4423680 | tf_op jit(solution)/shard_map/all_gather | solution.py:60
  9.4 477.2 %all-gather.14.cloned.1.call-start = ((), (), s32[]{:S(2)}) async-start(), calls=%async_computation.3 | async-start | bytes 4259840 | tf_op jit(solution)/shard_map/all_gather | solution.py:68
  360.6 3.5 copy-start
  360.6 3.9 copy-start.2
  365.7 15.5 %collective-permute-start.1 = (bf16[512,512]{0,1:T(8,128)(2,1)S(1)}, bf16[512,512]{0,1:T(8,128)(2,1)S(1)}, u32[]{:S(2)}, u32[]{:S(2)}) collective-permute-start(bf16[512,512]{0,1:T(8,128)(2,1)S(1)} %pad_maximum_fusion), channel_id=1, source_target_pairs={{0,8},{8,16},{16,24},{24,32},{32,40},{40,48},{48,56},{56,64},{64,7... | collective-permute-start | bytes 1572872 | tf_op jit(solution)/shard_map/ppermute | solution.py:13
  367.6 19.8 %collective-permute-start = (bf16[512,512]{0,1:T(8,128)(2,1)S(1)}, bf16[512,512]{0,1:T(8,128)(2,1)S(1)}, u32[]{:S(2)}, u32[]{:S(2)}) collective-permute-start(bf16[512,512]{0,1:T(8,128)(2,1)S(1)} %pad_maximum_fusion), channel_id=1, source_target_pairs={{0,16},{8,24},{16,32},{24,40},{32,48},{40,56},{48,64},{56,72},{64,... | collective-permute-start | bytes 1572872 | tf_op jit(solution)/shard_map/ppermute | solution.py:13
  499.7 1.3 copy-start.3
  506.1 8.5 %copy-start.1 = (f32[1536,1,256]{0,2,1:T(8,128)}, f32[1536,1,256]{0,2,1:T(8,128)S(1)}, u32[]{:S(2)}) copy-start(f32[1536,1,256]{0,2,1:T(8,128)S(1)} %fusion.13) | copy-start | bytes 4718596
  507.2 12.9 %collective-permute-start.2 = (f32[512,256]{0,1:T(8,128)}, f32[512,256]{0,1:T(8,128)S(1)}, u32[]{:S(2)}, u32[]{:S(2)}) collective-permute-start(f32[512,256]{0,1:T(8,128)} %get-tuple-element.10), channel_id=1, source_target_pairs={{8,0},{16,8},{24,16},{32,24},{40,32},{48,40},{56,48},{64,56},{72,6... | collective-permute-start | bytes 1572872 | tf_op jit(solution)/shard_map/ppermute | solution.py:13
  509.2 21.6 %collective-permute-start.3 = (f32[512,256]{0,1:T(8,128)}, f32[512,256]{0,1:T(8,128)S(1)}, u32[]{:S(2)}, u32[]{:S(2)}) collective-permute-start(f32[512,256]{0,1:T(8,128)} %get-tuple-element.11), channel_id=1, source_target_pairs={{16,0},{24,8},{32,16},{40,24},{48,32},{56,40},{64,48},{72,56},{80,... | collective-permute-start | bytes 1572872 | tf_op jit(solution)/shard_map/ppermute | solution.py:13
Sparse Core Ops, SparseCore 0:
  10.1 120.4 all-gather.9
  132.8 115.8 all-gather.11
  251.9 108.6 all-gather.7
  362.6 123.9 all-gather.13
where the time goes:
time: 540 us; the launch traced here: 539 us
  waiting for transfers between devices  472 us (87%)
  matrix products  19.5 us (4%)
  local copies, waits for them, and re-layouts  17.7 us (3%)
  between operations  13.9 us (3%)
  starting transfers between devices  11.3 us (2%)
    all_gather x1, waiting for transfers between devices, local(): key_sum = add_one(lax.all_gather(key_matrix, 'ctx', axis=0, tiled=True))  119 us
    all_gather x1, waiting for transfers between devices, local(): value_sum = add_one(lax.all_gather(value_matrix, 'ctx', axis=0, tiled=True))  116 us
    all_gather x1, waiting for transfers between devices, local(): features = lax.all_gather(tokens, 'head', axis=1, tiled=True)  108 us
    all_gather x1, waiting for transfers between devices, local(): query_sum = add_one(lax.all_gather(w_query, 'ctx', axis=0, tiled=True))  99 us
    ppermute x4, waiting for transfers between devices, from_behind(): return lax.ppermute(block, axis, route)  27.9 us
    unnamed x13, local copies, waits for them, and re-layouts  15.9 us
    ppermute x4, starting transfers between devices, from_behind(): return lax.ppermute(block, axis, route)  11.1 us
  transfers between devices with their start and end apart: 8, of which 8 were waited for; matrix products, arithmetic and copies ran while one was open for 4% of the time, Pallas kernels for 0%

commit v1 on v0

--- a/solution.py
+++ b/solution.py
@@ -57,6 +57,15 @@
 
 
 def local(tokens, w_query, key_matrix, value_matrix, d_attended, doc_lengths):
+
+    def step_on_tracks(chunk):
+        return jnp.concatenate(
+            jax.lax.all_to_all(
+                jnp.stack([chunk for _ in range(jax.lax.axis_size("ctx"))], axis=0), "ctx", 0, 0
+            ),
+            0,
+        )
+
     features = lax.all_gather(tokens, "head", axis=1, tiled=True)
     rows_here = features.shape[0]
     kv_width = key_matrix.shape[1]
@@ -65,7 +74,7 @@
     def add_one(piece):
         return add_rows(features, piece)
 
-    query_sum = add_one(lax.all_gather(w_query, "ctx", axis=0, tiled=True))
+    query_sum = add_one(step_on_tracks(w_query))
     key_sum = add_one(lax.all_gather(key_matrix, "ctx", axis=0, tiled=True))
     value_sum = add_one(lax.all_gather(value_matrix, "ctx", axis=0, tiled=True))
     query = (query_sum * 0.0625).astype(jnp.bfloat16)

time: 540 us -> 505 us (0.935)
  the two profiles are of different devices: /device:TPU:24 before, /device:TPU:56 now
where the time goes in v1:
time: 505 us; the launch traced here: 504 us
  waiting for transfers between devices  420 us (83%)
  starting transfers between devices  26.5 us (5%)
  local copies, waits for them, and re-layouts  20.5 us (4%)
  matrix products  19.5 us (4%)
  between operations  13.9 us (3%)
    all_gather x1, waiting for transfers between devices, local(): key_sum = add_one(lax.all_gather(key_matrix, 'ctx', axis=0, tiled=True))  168 us
    all_gather x1, waiting for transfers between devices, local(): value_sum = add_one(lax.all_gather(value_matrix, 'ctx', axis=0, tiled=True))  115 us
    all_gather x1, waiting for transfers between devices, local(): features = lax.all_gather(tokens, 'head', axis=1, tiled=True)  108 us
    ppermute x4, waiting for transfers between devices, from_behind(): return lax.ppermute(block, axis, route)  26.3 us
    ppermute x4, starting transfers between devices, from_behind(): return lax.ppermute(block, axis, route)  13.2 us
    all_to_all x1, starting transfers between devices, step_on_tracks(): jax.lax.all_to_all(jnp.stack([chunk for _ in range(jax.lax.axis_size('ctx...  13.2 us
    dot_general x3, matrix products, add_rows(): return jnp.dot(features, piece, preferred_element_type=jnp.float32)  10.3 us
  transfers between devices with their start and end apart: 8, of which 7 were waited for; matrix products, arithmetic and copies ran while one was open for 4% of the time, Pallas kernels for 0%

profile of v1, /device:TPU:56, one launch (start us, length us, event | category | flops | bytes accessed | tf_op | source)
XLA Modules:
  0.0 504.2 jit_solution(16954440286603299921)
XLA Ops:
  7.2 0.0 all-gather.8.cloned.1.call-start
  7.2 0.7 all-gather.8.cloned.1.call-update
  7.9 0.0 all-gather.10.cloned.1.call-start
  7.9 0.7 all-gather.10.cloned.1.call-update
  8.6 0.0 all-gather.6.cloned.1.call-start
  8.7 0.7 all-gather.6.cloned.1.call-update
  9.4 3.3 stack.2
  12.7 13.2 %all-to-all-start = ((bf16[64,60,512]{2,1,0:T(8,128)(2,1)}), bf16[64,60,512]{2,1,0:T(8,128)(2,1)}, u32[]{:S(2)}, u32[]{:S(2)}) async-start(bf16[64,60,512]{2,1,0:T(8,128)(2,1)} %stack.2), calls=%async_computation | async-start | bytes 8388608 | tf_op jit(solution)/shard_map/all_to_all | solution.py:63
  25.9 0.0 copy-done.2
  25.9 0.1 copy.35
  26.0 0.1 reduce-window.9
  26.0 0.1 reduce.3
  26.2 0.1 select_reduce_fusion
  26.3 168.2 %all-gather.8.cloned.1.call-done = bf16[64,60,256]{2,1,0:T(8,128)(2,1)} async-done(((bf16[1,60,256]{2,1,0:T(8,128)(2,1)}), bf16[64,60,256]{2,1,0:T(8,128)(2,1)}) %all-gather.8.cloned.1.call-update) | async-done | bytes 1966096 | tf_op jit(solution)/shard_map/all_gather | solution.py:78
  194.5 2.5 reshape.194
  197.0 115.1 %all-gather.10.cloned.1.call-done = bf16[64,60,256]{2,1,0:T(8,128)(2,1)} async-done(((bf16[1,60,256]{2,1,0:T(8,128)(2,1)}), bf16[64,60,256]{2,1,0:T(8,128)(2,1)}) %all-gather.10.cloned.1.call-update) | async-done | bytes 1966096 | tf_op jit(solution)/shard_map/all_gather | solution.py:79
  312.1 3.8 reshape.196
  315.9 108.0 %all-gather.6.cloned.1.call-done = bf16[512,3840]{0,1:T(8,128)(2,1)} async-done(((bf16[512,480]{0,1:T(8,128)(2,1)}), bf16[512,3840]{0,1:T(8,128)(2,1)}) %all-gather.6.cloned.1.call-update) | async-done | bytes 3932176 | tf_op jit(solution)/shard_map/all_gather | solution.py:69
  423.9 3.5 convolution_convert_fusion.1
  427.4 0.0 copy-done
  427.4 0.4 copy-done.3
  427.8 1.2 convolution_convert_fusion
  429.1 1.9 collective-permute-start.1
  431.0 2.1 collective-permute-start
  433.1 1.2 compare_and_fusion
  434.3 8.4 %collective-permute-done.1 = bf16[512,512]{0,1:T(8,128)(2,1)S(1)} collective-permute-done((bf16[512,512]{0,1:T(8,128)(2,1)S(1)}, bf16[512,512]{0,1:T(8,128)(2,1)S(1)}, u32[]{:S(2)}, u32[]{:S(2)}) %collective-permute-start.1) | collective-permute-done | bytes 524320 | tf_op jit(solution)/shard_map/ppermute | solution.py:13
  442.7 5.0 collective-permute-done
  447.7 0.1 maximum_maximum_fusion
  447.8 0.0 all-to-all-done
  447.8 6.4 %reshape.187 = bf16[3840,512]{1,0:T(8,128)(2,1)} reshape(bf16[64,60,512]{2,1,0:T(8,128)(2,1)} %all-to-all-done) | data formatting | bytes 7864320 | tf_op jit(solution)/shard_map/reshape | solution.py:62
  454.2 5.5 %fusion.21 = bf16[512,512]{0,1:T(8,128)(2,1)S(1)} fusion(bf16[512,3840]{0,1:T(8,128)(2,1)} %all-gather.6.cloned.1.call-done, bf16[3840,512]{1,0:T(8,128)(2,1)} %reshape.187), kind=kOutput, calls=%fused_computation.21 | convolution fusion | flops 2013790208 | bytes 8388608 | tf_op jit(solution)/shard_map/dot_general | solution.py:22
  459.8 1.3 fusion.3
  461.0 0.0 copy-start.4
  461.0 1.3 fusion.5
  462.3 0.0 copy-done.4
  462.4 2.5 fusion
  464.9 2.5 fusion.13
  467.4 0.0 copy-start.1
  467.4 1.1 slice_bitcast_fusion.6
  468.6 5.9 %collective-permute-start.2 = (f32[512,256]{0,1:T(8,128)}, f32[512,256]{0,1:T(8,128)S(1)}, u32[]{:S(2)}, u32[]{:S(2)}) collective-permute-start(f32[512,256]{0,1:T(8,128)} %get-tuple-element.10), channel_id=1, source_target_pairs={{8,0},{16,8},{24,16},{32,24},{40,32},{48,40},{56,48},{64,56},{72,6... | collective-permute-start | bytes 1572872 | tf_op jit(solution)/shard_map/ppermute | solution.py:13
  474.4 3.4 collective-permute-start.3
  477.8 3.0 fusion.18
  480.7 0.0 copy-done.1
  480.7 2.0 copy.42
  482.8 2.9 collective-permute-done.2
  485.7 10.0 %collective-permute-done.3 = f32[512,256]{0,1:T(8,128)S(1)} collective-permute-done((f32[512,256]{0,1:T(8,128)}, f32[512,256]{0,1:T(8,128)S(1)}, u32[]{:S(2)}, u32[]{:S(2)}) %collective-permute-start.3) | collective-permute-done | bytes 524320 | tf_op jit(solution)/shard_map/ppermute | solution.py:13
  495.7 1.2 fusion.28
  496.9 0.8 copy.43
  (7 shorter events, 0.1 us)
Async XLA Ops:
  7.2 187.3 %all-gather.8.cloned.1.call-start = ((), (), s32[]{:S(2)}) async-start(), calls=%async_computation.2 | async-start | bytes 2129920 | tf_op jit(solution)/shard_map/all_gather | solution.py:78
  7.9 304.2 %all-gather.10.cloned.1.call-start = ((), (), s32[]{:S(2)}) async-start(), calls=%async_computation.3 | async-start | bytes 2129920 | tf_op jit(solution)/shard_map/all_gather | solution.py:79
  8.6 415.3 %all-gather.6.cloned.1.call-start = ((), (), s32[]{:S(2)}) async-start(), calls=%async_computation.1 | async-start | bytes 4423680 | tf_op jit(solution)/shard_map/all_gather | solution.py:69
  12.7 13.2 %copy-start.2 = (s32[32]{0:T(128)S(1)}, s32[32]{0:T(128)}, u32[]{:S(2)}) copy-start(s32[32]{0:T(128)} %param.11) | copy-start | bytes 388
  12.7 435.1 %all-to-all-start = ((bf16[64,60,512]{2,1,0:T(8,128)(2,1)}), bf16[64,60,512]{2,1,0:T(8,128)(2,1)}, u32[]{:S(2)}, u32[]{:S(2)}) async-start(bf16[64,60,512]{2,1,0:T(8,128)(2,1)} %stack.2), calls=%async_computation | async-start | bytes 8388608 | tf_op jit(solution)/shard_map/all_to_all | solution.py:63
  423.9 3.5 copy-start
  423.9 3.9 copy-start.3
  429.1 13.6 %collective-permute-start.1 = (bf16[512,512]{0,1:T(8,128)(2,1)S(1)}, bf16[512,512]{0,1:T(8,128)(2,1)S(1)}, u32[]{:S(2)}, u32[]{:S(2)}) collective-permute-start(bf16[512,512]{0,1:T(8,128)(2,1)S(1)} %pad_maximum_fusion), channel_id=1, source_target_pairs={{0,8},{8,16},{16,24},{24,32},{32,40},{40,48},{48,56},{56,64},{64,7... | collective-permute-start | bytes 1572872 | tf_op jit(solution)/shard_map/ppermute | solution.py:13
  431.0 16.7 %collective-permute-start = (bf16[512,512]{0,1:T(8,128)(2,1)S(1)}, bf16[512,512]{0,1:T(8,128)(2,1)S(1)}, u32[]{:S(2)}, u32[]{:S(2)}) collective-permute-start(bf16[512,512]{0,1:T(8,128)(2,1)S(1)} %pad_maximum_fusion), channel_id=1, source_target_pairs={{0,16},{8,24},{16,32},{24,40},{32,48},{40,56},{48,64},{56,72},{64,... | collective-permute-start | bytes 1572872 | tf_op jit(solution)/shard_map/ppermute | solution.py:13
  461.0 1.3 copy-start.4
  467.4 13.3 %copy-start.1 = (f32[1536,1,256]{0,2,1:T(8,128)}, f32[1536,1,256]{0,2,1:T(8,128)S(1)}, u32[]{:S(2)}) copy-start(f32[1536,1,256]{0,2,1:T(8,128)S(1)} %fusion.13) | copy-start | bytes 4718596
  468.6 17.1 %collective-permute-start.2 = (f32[512,256]{0,1:T(8,128)}, f32[512,256]{0,1:T(8,128)S(1)}, u32[]{:S(2)}, u32[]{:S(2)}) collective-permute-start(f32[512,256]{0,1:T(8,128)} %get-tuple-element.10), channel_id=1, source_target_pairs={{8,0},{16,8},{24,16},{32,24},{40,32},{48,40},{56,48},{64,56},{72,6... | collective-permute-start | bytes 1572872 | tf_op jit(solution)/shard_map/ppermute | solution.py:13
  474.4 21.3 %collective-permute-start.3 = (f32[512,256]{0,1:T(8,128)}, f32[512,256]{0,1:T(8,128)S(1)}, u32[]{:S(2)}, u32[]{:S(2)}) collective-permute-start(f32[512,256]{0,1:T(8,128)} %get-tuple-element.11), channel_id=1, source_target_pairs={{16,0},{24,8},{32,16},{40,24},{48,32},{56,40},{64,48},{72,56},{80,... | collective-permute-start | bytes 1572872 | tf_op jit(solution)/shard_map/ppermute | solution.py:13
Sparse Core Ops, SparseCore 0:
  10.1 184.3 all-gather.7
  196.7 115.4 all-gather.9
  315.3 108.5 all-gather.5
